TPU v7x, 32 devices: a whole 2x2x4 slice. The times are simulated.
32 devices in a mesh: dp: 8 (over z, x), tensor: 4 (over y, core).
Axes of the slice: x: 2, y: 2, z: 4, core: 2. Of those that a mesh axis runs over, the one named last changes fastest.
Arguments:
- patches: bfloat16 [192, 196, 768], P('dp'), may hold values from -6 to 6
- keep_slots: int32 [192, 98], P('dp'), may hold values from 0 to 195, as said below
- visible_count: int32 [192], P('dp'), may hold values from 39 to 98, as said below
- gain_one: float32 [768], replicated, may hold values from 0.1 to 1.9
- shift_one: float32 [768], replicated, may hold values from -4 to 4
- w_qkv: bfloat16 [3, 768, 768], P(None, None, 'tensor'), may hold values from -0.21875 to 0.21875
- b_qv: float32 [2, 768], P(None, 'tensor'), may hold values from -4 to 4
- w_out: bfloat16 [768, 768], P('tensor'), may hold values from -1.75 to 1.75
- b_out: float32 [768], replicated, may hold values from -4 to 4
- gain_two: float32 [768], replicated, may hold values from 0.1 to 1.9
- shift_two: float32 [768], replicated, may hold values from -4 to 4
- w_fc1: bfloat16 [768, 3072], P(None, 'tensor'), may hold values from -0.21875 to 0.21875
- b_fc1: float32 [3072], P('tensor'), may hold values from -4 to 4
- w_fc2: bfloat16 [3072, 768], P('tensor'), may hold values from -0.109375 to 0.109375
- b_fc2: float32 [768], replicated, may hold values from -4 to 4
- out_grad: bfloat16 [192, 98, 768], P(('dp', 'tensor')), may hold values from -6 to 6
Outputs:
- layer_out: bfloat16 [192, 98, 768], P(('dp', 'tensor'))
- grad_patches: float32 [192, 196, 768], P(('dp', 'tensor'))
- grad_gain_one: float32 [768], replicated
- grad_shift_one: float32 [768], replicated
- grad_w_qkv: float32 [3, 768, 768], P(None, None, 'tensor')
- grad_b_qv: float32 [2, 768], P(None, 'tensor')
- grad_w_out: float32 [768, 768], P('tensor')
- grad_b_out: float32 [768], replicated
- grad_gain_two: float32 [768], replicated
- grad_shift_two: float32 [768], replicated
- grad_w_fc1: float32 [768, 3072], P(None, 'tensor')
- grad_b_fc1: float32 [3072], P('tensor')
- grad_w_fc2: float32 [3072, 768], P('tensor')
- grad_b_fc2: float32 [768], replicated
Inputs may be any that keep to these rules, and one draw needn't show every extreme that they name: `visible_count`: visible patches of each image; in every draw some image has 98 and some has 196 // 5. `keep_slots`: the entries of a row are distinct patch indices of the image; the first visible_count of them are its visible patches, the others are ignored.
All inputs are finite; a program needn't handle non-finite values.
Results may differ from a plain program's by a relative error of at most 0.012.
The roundings to bfloat16 on the way count: a program that leaves them out, or rounds other values in their place, can miss the bound.
Values may be sent and summed in bfloat16 or wider, within the bound.
No kernel may reach another device: no remote copies, remote signals or barrier semaphores. Data moves between devices by JAX's collectives and lax.ppermute only.
A program may use at most 192 MiB of HBM per device.

v0:
```python
import jax
import jax.numpy as jnp
from jax import lax
from jax.sharding import PartitionSpec as P

HD = 64


EPSILON = 1e-06
MASKED = -1000000000.0


def standard(inputs):
    average = jnp.mean(inputs, axis=-1, keepdims=True)
    centered = inputs - average
    spread = jnp.mean(centered * centered, axis=-1, keepdims=True)
    return centered * lax.rsqrt(spread + EPSILON)


def affine_norm(inputs, weights, offsets):
    return standard(inputs) * weights + offsets


def norm_back(inputs, weights, offsets, gradient):
    _, backward = jax.vjp(affine_norm, inputs, weights, offsets)
    return backward(gradient)


def exact_gelu(values):
    return jax.nn.gelu(values, approximate=False)


def shards(
    patches,
    keep_slots,
    visible_count,
    gain_one,
    shift_one,
    w_qkv,
    b_qv,
    w_out,
    b_out,
    gain_two,
    shift_two,
    w_fc1,
    b_fc1,
    w_fc2,
    b_fc2,
    out_grad,
):
    images, slots = keep_slots.shape
    share = images // lax.axis_size("tensor")
    begin = lax.axis_index("tensor") * share
    visible = jnp.arange(slots, dtype=jnp.int32)[None, :] < visible_count[:, None]
    mask_share = lax.dynamic_slice_in_dim(visible, begin, share, 0)[:, :, None].astype(jnp.float32)
    tokens = jnp.take_along_axis(patches, keep_slots[:, :, None], axis=1).astype(jnp.float32)
    token_share = lax.dynamic_slice_in_dim(tokens, begin, share, 0)
    first = affine_norm(tokens, gain_one, shift_one).astype(jnp.bfloat16)
    projected = jnp.einsum("ivd,sdh->sivh", first, w_qkv, preferred_element_type=jnp.float32)
    local_heads = w_qkv.shape[2] // HD
    heads_shape = (images, slots, local_heads, HD)
    queries = (projected[0] + b_qv[0]).astype(jnp.bfloat16).reshape(heads_shape)
    keyset = projected[1].astype(jnp.bfloat16).reshape(heads_shape)
    valueset = (projected[2] + b_qv[1]).astype(jnp.bfloat16).reshape(heads_shape)
    factor = HD ** (-0.5)
    key_visible = visible[:, None, None, :]

    def scores_of(query_part, key_part):
        raw_scores = (
            jnp.einsum("iqhe,ikhe->ihqk", query_part, key_part, preferred_element_type=jnp.float32)
            * factor
        )
        return jnp.where(key_visible, raw_scores, MASKED)

    scores = scores_of(queries, keyset)
    highest = jnp.max(scores, axis=-1, keepdims=True)
    logsum = highest + jnp.log(jnp.sum(jnp.exp(scores - highest), axis=-1, keepdims=True))
    attention = jnp.exp(scores - logsum).astype(jnp.bfloat16)
    attended = jnp.einsum(
        "ihqk,ikhe->iqhe", attention, valueset, preferred_element_type=jnp.float32
    )
    attended = attended.astype(jnp.bfloat16).reshape(images, slots, local_heads * HD)
    branch_part = jnp.einsum("ivc,cd->ivd", attended, w_out, preferred_element_type=jnp.float32)
    middle = tokens + lax.psum(branch_part, "tensor") + b_out
    middle_share = lax.dynamic_slice_in_dim(middle, begin, share, 0)
    second = affine_norm(middle, gain_two, shift_two).astype(jnp.bfloat16)
    inner = jnp.einsum("ivd,df->ivf", second, w_fc1, preferred_element_type=jnp.float32) + b_fc1
    hidden_values, gelu_back = jax.vjp(exact_gelu, inner)
    hidden = hidden_values.astype(jnp.bfloat16)
    mlp_part = jnp.einsum("ivf,fd->ivd", hidden, w_fc2, preferred_element_type=jnp.float32)
    mlp_share = lax.psum_scatter(
        mlp_part.astype(jnp.bfloat16), "tensor", scatter_dimension=0, tiled=True
    ).astype(jnp.float32)
    layer_out = ((middle_share + mlp_share + b_fc2) * mask_share).astype(jnp.bfloat16)
    grad_share = out_grad.astype(jnp.float32) * mask_share
    grad_b_fc2 = jnp.sum(grad_share, axis=(0, 1))
    grad_rows = lax.all_gather(grad_share.astype(jnp.bfloat16), "tensor", axis=0, tiled=True)
    grad_w_fc2 = jnp.einsum("ivf,ivd->fd", hidden, grad_rows, preferred_element_type=jnp.float32)
    grad_hidden = jnp.einsum("ivd,fd->ivf", grad_rows, w_fc2, preferred_element_type=jnp.float32)
    grad_inner = gelu_back(grad_hidden)[0].astype(jnp.bfloat16)
    grad_b_fc1 = jnp.sum(grad_inner, axis=(0, 1), dtype=jnp.float32)
    grad_w_fc1 = jnp.einsum("ivd,ivf->df", second, grad_inner, preferred_element_type=jnp.float32)
    second_part = jnp.einsum("ivf,df->ivd", grad_inner, w_fc1, preferred_element_type=jnp.float32)
    grad_second = lax.psum(second_part, "tensor")
    _, middle_back = jax.vjp(lambda inputs: affine_norm(inputs, gain_two, shift_two), middle)
    grad_middle = grad_rows.astype(jnp.float32) + middle_back(grad_second)[0]
    grad_second_share = lax.dynamic_slice_in_dim(grad_second, begin, share, 0)
    grad_gain_two = jnp.sum(grad_second_share * standard(middle_share), axis=(0, 1))
    grad_shift_two = jnp.sum(grad_second_share, axis=(0, 1))
    grad_middle_share = lax.dynamic_slice_in_dim(grad_middle, begin, share, 0)
    grad_middle_rows = grad_middle.astype(jnp.bfloat16)
    grad_b_out = jnp.sum(grad_middle_share, axis=(0, 1))
    grad_w_out = jnp.einsum(
        "ivc,ivd->cd", attended, grad_middle_rows, preferred_element_type=jnp.float32
    )
    grad_attended = jnp.einsum(
        "ivd,cd->ivc", grad_middle_rows, w_out, preferred_element_type=jnp.float32
    )
    grad_attended = grad_attended.astype(jnp.bfloat16).reshape(heads_shape)
    again = scores_of(queries, keyset)
    prob_exact = jnp.exp(again - logsum)
    prob_round = prob_exact.astype(jnp.bfloat16)
    grad_prob = jnp.einsum(
        "iqhe,ikhe->ihqk", grad_attended, valueset, preferred_element_type=jnp.float32
    )
    grad_scores = prob_exact * (grad_prob - jnp.sum(prob_exact * grad_prob, axis=-1, keepdims=True))
    grad_scores = grad_scores.astype(jnp.bfloat16)
    grad_queries = (
        jnp.einsum("ihqk,ikhe->iqhe", grad_scores, keyset, preferred_element_type=jnp.float32)
        * factor
    ).astype(jnp.bfloat16)
    grad_keys = (
        jnp.einsum("ihqk,iqhe->ikhe", grad_scores, queries, preferred_element_type=jnp.float32)
        * factor
    ).astype(jnp.bfloat16)
    grad_values = jnp.einsum(
        "ihqk,iqhe->ikhe", prob_round, grad_attended, preferred_element_type=jnp.float32
    ).astype(jnp.bfloat16)
    grad_projected = jnp.stack([grad_queries, grad_keys, grad_values]).reshape(
        3, images, slots, local_heads * HD
    )
    grad_b_qv = jnp.stack(
        [
            jnp.sum(grad_projected[0], axis=(0, 1), dtype=jnp.float32),
            jnp.sum(grad_projected[2], axis=(0, 1), dtype=jnp.float32),
        ]
    )
    grad_w_qkv = jnp.einsum(
        "ivd,sivh->sdh", first, grad_projected, preferred_element_type=jnp.float32
    )
    first_part = jnp.einsum(
        "sivh,sdh->ivd", grad_projected, w_qkv, preferred_element_type=jnp.float32
    )
    grad_first_share = lax.psum_scatter(first_part, "tensor", scatter_dimension=0, tiled=True)
    token_grad, grad_gain_one, grad_shift_one = norm_back(
        token_share, gain_one, shift_one, grad_first_share
    )
    grad_tokens = grad_middle_share + token_grad
    slot_share = lax.dynamic_slice_in_dim(keep_slots, begin, share, 0)
    image_rows = jnp.arange(share, dtype=jnp.int32)[:, None]
    grad_patches = (
        jnp.zeros((share, patches.shape[1], patches.shape[2]), jnp.float32)
        .at[image_rows, slot_share]
        .add(grad_tokens)
    )
    grad_w_qkv, grad_b_qv, grad_w_out, grad_w_fc1, grad_b_fc1, grad_w_fc2 = lax.psum(
        (grad_w_qkv, grad_b_qv, grad_w_out, grad_w_fc1, grad_b_fc1, grad_w_fc2), "dp"
    )
    grad_gain_one, grad_shift_one, grad_b_out, grad_gain_two, grad_shift_two, grad_b_fc2 = lax.psum(
        (grad_gain_one, grad_shift_one, grad_b_out, grad_gain_two, grad_shift_two, grad_b_fc2),
        ("dp", "tensor"),
    )
    return (
        layer_out,
        grad_patches,
        grad_gain_one,
        grad_shift_one,
        grad_w_qkv,
        grad_b_qv,
        grad_w_out,
        grad_b_out,
        grad_gain_two,
        grad_shift_two,
        grad_w_fc1,
        grad_b_fc1,
        grad_w_fc2,
        grad_b_fc2,
    )


def solution(mesh):
    return jax.shard_map(
        shards,
        mesh=mesh,
        in_specs=(
            P("dp", None, None),
            P("dp", None),
            P("dp"),
            P(),
            P(),
            P(None, None, "tensor"),
            P(None, "tensor"),
            P("tensor", None),
            P(),
            P(),
            P(),
            P(None, "tensor"),
            P("tensor"),
            P("tensor", None),
            P(),
            P(("dp", "tensor"), None, None),
        ),
        out_specs=(
            P(("dp", "tensor"), None, None),
            P(("dp", "tensor"), None, None),
            P(),
            P(),
            P(None, None, "tensor"),
            P(None, "tensor"),
            P("tensor", None),
            P(),
            P(),
            P(),
            P(None, "tensor"),
            P("tensor"),
            P("tensor", None),
            P(),
        ),
        check_vma=False,
    )
```

profile of v0, /device:TPU:0, one launch (start us, length us, event | category | flops | bytes accessed | tf_op | source)
XLA Modules:
  0.0 807.7 jit_solution(15770494399392824385)
XLA Ops:
  8.9 41.4 %gather_fusion = bf16[2352,768]{1,0:T(8,128)(2,1)} fusion(bf16[24,196,768]{2,0,1:T(8,128)(2,1)} %param.16, s32[2352]{0:T(1024)S(1)} %reshape.192), kind=kCustom, calls=%fused_computation | custom fusion | bytes 7244160 | tf_op jit(solution)/shard_map/jit(take_along_axis)/gather | solution.py:56
  50.3 5.8 reshape.195
  78.4 4.3 fusion.36
  86.2 141.4 %all-reduce.7.cloned.1.call-done = f32[24,98,768]{2,1,0:T(8,128)} async-done(((f32[24,98,768]{2,1,0:T(8,128)}), f32[24,98,768]{2,1,0:T(8,128)}) %all-reduce.7.cloned.1.call-update) | async-done | bytes 7225360 | tf_op jit(solution)/shard_map/psum | solution.py:84
  227.6 5.3 fusion.57
  236.0 6.4 convert_reduce_fusion.1
  245.5 18.4 %multiply_convert_fusion = (bf16[24,98,768]{2,1,0:T(8,128)(2,1)}, f32[24,98,768]{2,1,0:T(8,128)}) fusion(f32[24,98,768]{2,1,0:T(8,128)S(1)} %get-tuple-element.52, f32[768]{0:T(1024)S(1)} %copy-done.56, u32[98,768]{1,0:T(8,128)S(1)} %get-tuple-element.19, u32[98,768]{1,0:T(8,128)S(1)} %get-tuple-element.18), kind=kLoop, calls=%fused_computation.14 | loop fusion | flops 124637184 | bytes 18668544 | tf_op jit(solution)/shard_map/convert_element_type | solution.py:89
  263.9 11.6 %convert_reduce_fusion.2 = (f32[768]{0:T(1024)}, bf16[24,98,768]{2,1,0:T(8,128)(2,1)S(1)}) fusion(f32[24,98,768]{2,1,0:T(8,128)} %get-tuple-element.38, bf16[24,98,768]{2,1,0:T(8,128)(2,1)} %all-gather.2.cloned.1.call-done, bf16[768,768]{1,0:T(8,128)(2,1)} %param.29, f32[24,98,768]{2,1,0:T(8,128)} %copy-done.16, f32[768]{0:T(1024)} %param.28), kind=kOutput, calls=%fused_computation.10 | convolution fusion | flops 2805239040 | bytes 22861824 | tf_op jit(solution)/shard_map/ivd,fd->ivf/dot_general | solution.py:99
  277.3 15.7 %fusion.24 = f32[24,98,768]{2,1,0:T(8,128)} fusion(bf16[24,98,768]{2,1,0:T(8,128)(2,1)S(1)} %get-tuple-element.60, bf16[768,768]{1,0:T(8,128)(2,1)S(1)} %copy-done), kind=kOutput, calls=%fused_computation.83 | convolution fusion | flops 2774532096 | bytes 12017664 | tf_op jit(solution)/shard_map/ivf,df->ivd/dot_general | solution.py:103
  294.3 7.1 convolution_convert_fusion
  301.6 133.9 %all-reduce.9.cloned.1.call-done = f32[24,98,768]{2,1,0:T(8,128)} async-done(((f32[24,98,768]{2,1,0:T(8,128)}), f32[24,98,768]{2,1,0:T(8,128)}) %all-reduce.9.cloned.1.call-update) | async-done | bytes 7225360 | tf_op jit(solution)/shard_map/psum | solution.py:104
  435.5 6.4 multiply_reduce_fusion
  443.1 6.5 fusion.28
  467.5 5.4 convolution_bitcast_fusion
  473.3 8.2 %convolution_bitcast_fusion.2 = f32[768,768]{1,0:T(8,128)} fusion(bf16[24,98,768]{2,1,0:T(8,128)(2,1)} %get-tuple-element.37, bf16[24,98,768]{2,1,0:T(8,128)(2,1)} %all-gather.2.cloned.1.call-done), kind=kOutput, calls=%fused_computation.73 | convolution fusion | flops 2774532096 | bytes 9584640 | tf_op jit(solution)/shard_map/ivf,ivd->fd/dot_general | solution.py:98
  481.5 8.8 %convolution_bitcast_fusion.3 = f32[768,768]{1,0:T(8,128)} fusion(bf16[24,98,768]{2,1,0:T(8,128)(2,1)S(1)} %copy-done.66, f32[24,98,768]{2,1,0:T(8,128)} %copy-done.2, f32[768]{0:T(1024)S(1)} %copy-done.62, f32[768]{0:T(1024)S(1)} %copy-done.42, f32[24,98]{1,0:T(8,128)S(1)} %copy-done.33, f32[24,98]{1,0:T(8,128)S(1)} %broadcast_multiply_fusion), kind=kOutput, calls=%fused_computation.74 | convolution fusion | flops 2783563776 | bytes 13222272 | tf_op jit(solution)/shard_map/ivd,ivf->df/dot_general | solution.py:102
  494.9 5.7 convolution_bitcast_fusion.4
  512.0 22.0 %all-reduce.1 = (f32[2,192]{1,0:T(2,128)}, f32[768]{0:T(1024)}) all-reduce(f32[2,192]{1,0:T(2,128)S(1)} %pad_maximum_fusion.3, f32[768]{0:T(1024)S(1)} %copy-done.58), channel_id=1, replica_groups=mesh['dp'=8,'tensor'=4] {'dp'}, use_global_device_ids=true, to_apply=%region_25.26 | all-reduce | flops 1152 | bytes 9216 | tf_op jit(solution)/shard_map/psum | solution.py:166
  534.0 3.9 dynamic-slice_reduce_fusion
  537.9 12.8 %reduce-scatter.5.cloned.1.call-done = f32[6,98,768]{2,1,0:T(8,128)} async-done(((f32[24,98,768]{2,1,0:T(8,128)}), f32[6,98,768]{2,1,0:T(8,128)}) %reduce-scatter.5.cloned.1.call-update) | async-done | bytes 1806352 | tf_op jit(solution)/shard_map/reduce_scatter | solution.py:154
  556.1 4.0 dynamic-slice_reduce_fusion.2
  564.0 81.4 %scatter_fusion = f32[6,196,768]{2,1,0:T(8,128)} fusion(f32[6,196,768]{2,1,0:T(8,128)} %broadcast_in_dim.42, s32[588]{0:T(1024)S(1)} %reshape.198, f32[588,768]{1,0:T(8,128)S(1)} %reshape.200), kind=kCustom, calls=%fused_computation.1 | custom fusion | flops 451584 | bytes 5423712 | tf_op jit(solution)/shard_map/scatter-add | solution.py:164
  645.3 41.0 %all-reduce = (f32[768]{0:T(1024)}, f32[768]{0:T(1024)}, f32[768]{0:T(1024)}, f32[768]{0:T(1024)}, f32[768]{0:T(1024)}, /*index=5*/f32[768]{0:T(1024)}) all-reduce(f32[768]{0:T(1024)S(1)} %get-tuple-element.14, f32[768]{0:T(1024)S(1)} %get-tuple-element.22, ...), channel_id=1, replica_groups=mesh['dp'=8,'tensor'=4] {'dp','tensor'}, use_global_device_ids=true, to_apply=%region_19.20 | all-reduce | flops 4608 | bytes 36864 | tf_op jit(solution)/shard_map/psum | solution.py:169
  686.3 107.6 %all-reduce.11.cloned.1.call-done = (f32[3,768,192]{1,2,0:T(8,128)}, f32[192,768]{1,0:T(8,128)}, f32[768,768]{1,0:T(8,128)}, f32[768,768]{1,0:T(8,128)}) async-done(((f32[3,768,192]{1,2,0:T(8,128)}, f32[192,768]{1,0:T(8,128)}, f32[768,768]{1,0:T(8,128)}, f32[768,768]{1,0:T(8,128)}), (f32[3,768,192]{1,2,0:T(8,128)}, f32[192,768]{1,0:T(8,128)}, f32[768,768]{1,0:T(8,128)}, ...) | async-done | bytes 7077904 | tf_op jit(solution)/shard_map/psum | solution.py:166
  (213 shorter events, 87.1 us)
Async XLA Ops:
  7.2 228.8 %copy-start = (bf16[768,768]{1,0:T(8,128)(2,1)S(1)}, bf16[768,768]{1,0:T(8,128)(2,1)}, u32[]{:S(2)}) copy-start(bf16[768,768]{1,0:T(8,128)(2,1)} %param.27) | copy-start | bytes 3538948
  7.2 220.4 %all-reduce.7.cloned.1.call-start = ((), (), s32[]{:S(2)}) async-start(), calls=%async_computation.2 | async-start | bytes 15335424 | tf_op jit(solution)/shard_map/psum | solution.py:84
  8.8 218.8 %copy-start.36 = (pred[24,98]{1,0:T(8,128)(4,1)}, pred[24,98]{1,0:T(8,128)(4,1)S(1)}, u32[]{:S(2)}) copy-start(pred[24,98]{1,0:T(8,128)(4,1)S(1)} %compare_and_fusion) | copy-start | bytes 7060
  82.7 144.8 %copy-start.55 = (f32[768]{0:T(1024)S(1)}, f32[768]{0:T(1024)}, u32[]{:S(2)}) copy-start(f32[768]{0:T(1024)} %param.24) | copy-start | bytes 9220
  82.7 181.2 %all-gather.2.cloned.1.call-start = ((), (), s32[]{:S(2)}) async-start(), calls=%async_computation.4 | async-start | bytes 4792320 | tf_op jit(solution)/shard_map/all_gather | solution.py:97
  83.1 149.8 %copy-start.43 = (f32[6,98]{1,0:T(8,128)}, f32[6,98]{1,0:T(8,128)S(1)}, u32[]{:S(2)}) copy-start(f32[6,98]{1,0:T(8,128)S(1)} %dynamic-slice_convert_fusion) | copy-start | bytes 7060
  86.1 349.4 %all-reduce.9.cloned.1.call-start = ((), (), s32[]{:S(2)}) async-start(), calls=%async_computation.5 | async-start | bytes 15335424 | tf_op jit(solution)/shard_map/psum | solution.py:104
  293.1 240.9 %reduce-scatter.3.cloned.1.call-start = ((), (), s32[]{:S(2)}) async-start(), calls=%async_computation.3 | async-start | bytes 4792320 | tf_op jit(solution)/shard_map/reduce_scatter | solution.py:91
  301.5 134.0 %copy-start.41 = (f32[768]{0:T(1024)S(1)}, f32[768]{0:T(1024)}, u32[]{:S(2)}) copy-start(f32[768]{0:T(1024)} %param.25) | copy-start | bytes 9220
  301.5 140.4 %copy-start.35 = (f32[24,98]{1,0:T(8,128)S(1)}, f32[24,98]{1,0:T(8,128)}, u32[]{:S(2)}) copy-start(f32[24,98]{1,0:T(8,128)} %copy-done.34) | copy-start | bytes 28228
  301.5 140.4 %copy-start.32 = (f32[24,98]{1,0:T(8,128)S(1)}, f32[24,98]{1,0:T(8,128)}, u32[]{:S(2)}) copy-start(f32[24,98]{1,0:T(8,128)} %copy-done.31) | copy-start | bytes 28228
  301.5 249.2 %reduce-scatter.5.cloned.1.call-start = ((), (), s32[]{:S(2)}) async-start(), calls=%async_computation.6 | async-start | bytes 9584640 | tf_op jit(solution)/shard_map/reduce_scatter | solution.py:154
  435.5 14.1 %slice-start = ((s8[7667712]{0:T(1024)(128)(4,1)}), s8[4194304]{0:T(1024)(128)(4,1)S(1)}, s32[]{:S(2)}) async-start(s8[7667712]{0:T(1024)(128)(4,1)} %bitcast.93), calls=%async_computation.8 | async-start | bytes 8388608
  473.0 8.5 %copy-start.33 = (f32[24,98]{1,0:T(8,128)S(1)}, f32[24,98]{1,0:T(8,128)}, u32[]{:S(2)}) copy-start(f32[24,98]{1,0:T(8,128)} %copy-done.31) | copy-start | bytes 28228
  473.0 8.5 %copy-start.42 = (f32[768]{0:T(1024)S(1)}, f32[768]{0:T(1024)}, u32[]{:S(2)}) copy-start(f32[768]{0:T(1024)} %param.25) | copy-start | bytes 9220
  473.0 8.5 %copy-start.62 = (f32[768]{0:T(1024)S(1)}, f32[768]{0:T(1024)}, u32[]{:S(2)}) copy-start(f32[768]{0:T(1024)} %param.26) | copy-start | bytes 9220
  473.0 320.8 %all-reduce.11.cloned.1.call-start = ((), (), s32[]{:S(2)}) async-start(), calls=%async_computation.7 | async-start | bytes 14155776 | tf_op jit(solution)/shard_map/psum | solution.py:166
  473.3 8.2 %copy-start.66 = (bf16[24,98,768]{2,1,0:T(8,128)(2,1)S(1)}, bf16[24,98,768]{2,1,0:T(8,128)(2,1)}, u32[]{:S(2)}) copy-start(bf16[24,98,768]{2,1,0:T(8,128)(2,1)} %copy-done.65) | copy-start | bytes 10838020
  473.3 17.0 %slice-start.2 = ((s8[7667712]{0:T(1024)(128)(4,1)}), s8[4194304]{0:T(1024)(128)(4,1)S(1)}, s32[]{:S(2)}) async-start(s8[7667712]{0:T(1024)(128)(4,1)} %bitcast.95), calls=%async_computation.10 | async-start | bytes 8388608
  481.5 8.8 %slice-start.3 = ((s8[7667712]{0:T(1024)(128)(4,1)}), s8[3473408]{0:T(1024)(128)(4,1)S(1)}, s32[]{:S(2)}) async-start(s8[7667712]{0:T(1024)(128)(4,1)} %bitcast.95), calls=%async_computation.11 | async-start | bytes 6946816
  481.5 8.8 %copy-start.14 = (bf16[24,3,64,98]{3,2,1,0:T(8,128)(2,1)S(1)}, bf16[24,3,64,98]{3,2,1,0:T(8,128)(2,1)}, u32[]{:S(2)}) copy-start(bf16[24,3,64,98]{3,2,1,0:T(8,128)(2,1)} %copy-done.13) | copy-start | bytes 2709508
  507.9 26.0 %copy-start.44 = (f32[6,98]{1,0:T(8,128)S(1)}, f32[6,98]{1,0:T(8,128)}, u32[]{:S(2)}) copy-start(f32[6,98]{1,0:T(8,128)} %copy-done.43) | copy-start | bytes 7060
  507.9 26.0 %copy-start.57 = (f32[768]{0:T(1024)S(1)}, f32[768]{0:T(1024)}, u32[]{:S(2)}) copy-start(f32[768]{0:T(1024)} %param.30) | copy-start | bytes 9220
  563.9 81.4 %copy-start.51 = (f32[768]{0:T(1024)S(1)}, f32[768]{0:T(1024)}, u32[]{:S(2)}) copy-start(f32[768]{0:T(1024)} %get-tuple-element.46) | copy-start | bytes 9220
  (53 other events, 213.3 us)
Sparse Core Ops, SparseCore 0:
  82.9 144.6 all-reduce.6
  229.8 32.6 all-gather.1
  293.2 142.2 all-reduce.8
  437.9 42.5 reduce-scatter.2
  483.0 67.6 reduce-scatter.4
  556.2 237.6 all-reduce.10
where the time goes:
time: 820 us; the launch traced here: 808 us
  waiting for transfers between devices  396 us (48%)
  other arithmetic  156 us (19%)
  matrix products  91 us (11%)
  local copies, waits for them, and re-layouts  85.9 us (10%)
  blocking collectives  63 us (8%)
  between operations  15.4 us (2%)
    psum x1, waiting for transfers between devices, shards(): middle = tokens + lax.psum(branch_part, 'tensor') + b_out  141 us
    psum x1, waiting for transfers between devices, shards(): grad_second = lax.psum(second_part, 'tensor')  134 us
    psum x1, waiting for transfers between devices, shards(): lax.psum((grad_w_qkv, grad_b_qv, grad_w_out, grad_w_fc1, grad_b_fc1, grad...  108 us
    scatter-add x1, other arithmetic, shards(): grad_patches = jnp.zeros((share, patches.shape[1], patches.shape[2]), jnp...  81.4 us
    gather x3, local copies, waits for them, and re-layouts, shards(): jnp.take_along_axis(patches, keep_slots[:, :, None], axis=1)  47.4 us
    psum x1, blocking collectives, shards(): lax.psum((grad_gain_one, grad_shift_one, grad_b_out, grad_gain_two, grad_...  41 us
    unnamed x146, local copies, waits for them, and re-layouts  30.1 us
    psum x1, blocking collectives, shards(): lax.psum((grad_w_qkv, grad_b_qv, grad_w_out, grad_w_fc1, grad_b_fc1, grad...  22 us
  transfers between devices with their start and end apart: 6, of which 4 were waited for; matrix products, arithmetic and copies ran while one was open for 25% of the time, Pallas kernels for 0%

commit v1 on v0

v1 whole, which is shorter than its diff:
```python
import functools

import jax
import jax.numpy as jnp
from jax import lax
from jax.experimental import pallas as pl
from jax.experimental.pallas import tpu as pltpu
from jax.sharding import PartitionSpec as P

HD = 64
EPSILON = 1e-06
MASKED = -1000000000.0
F32 = jnp.float32
BF16 = jnp.bfloat16
VMEM = pltpu.VMEM
NN = (((1,), (0,)), ((), ()))
NT = (((1,), (1,)), ((), ()))
TN = (((0,), (0,)), ((), ()))


def dot(left, right, dims=NN):
    return lax.dot_general(left, right, dims, preferred_element_type=F32)


def standard(inputs):
    average = jnp.mean(inputs, axis=-1, keepdims=True)
    centered = inputs - average
    spread = jnp.mean(centered * centered, axis=-1, keepdims=True)
    inverse = lax.rsqrt(spread + EPSILON)
    return centered * inverse, inverse


def norm_back(normal, inverse, gain, gradient):
    scaled = gradient * gain
    first = jnp.mean(scaled, axis=-1, keepdims=True)
    second = jnp.mean(scaled * normal, axis=-1, keepdims=True)
    return inverse * (scaled - first - normal * second)


def slots_matrix(keep_row, patch_count):
    places = lax.broadcasted_iota(jnp.int32, (patch_count, keep_row.shape[1]), 0)
    return (places == keep_row).astype(F32).astype(BF16)


def add_row(ref, value):
    row = jnp.sum(value, axis=0, keepdims=True)

    @pl.when(pl.program_id(0) == 0)
    def _():
        ref[...] = jnp.zeros_like(ref)

    ref[...] += row


def full(shape):
    return pl.BlockSpec(shape, lambda i, *_: (0,) * len(shape))


def rows(count, width):
    return pl.BlockSpec((count, width), lambda i, *_: (i, 0))


def call(body, grid, scalars, ins, in_specs, outs, out_specs, scratch=(), flops=0, alias=None):
    size = sum(a.size * a.dtype.itemsize for a in ins)
    size += sum(o.size * o.dtype.itemsize for o in outs)
    return pl.pallas_call(
        body,
        out_shape=outs,
        grid_spec=pltpu.PrefetchScalarGridSpec(
            num_scalar_prefetch=len(scalars),
            grid=grid,
            in_specs=in_specs,
            out_specs=out_specs,
            scratch_shapes=scratch,
        ),
        compiler_params=pltpu.CompilerParams(vmem_limit_bytes=50 * 2**20),
        input_output_aliases=alias or {},
        cost_estimate=pl.CostEstimate(flops=100 * flops, bytes_accessed=100 * size, transcendentals=0),
    )(*scalars, *ins)


def shape_of(shape, kind):
    return jax.ShapeDtypeStruct(shape, kind)


def prepare(place, counts, keep, patches, out_grad, gain, shift, slots):
    share, padded, width = out_grad.shape[0], keep.shape[1], patches.shape[2]
    patch_count = patches.shape[1]
    total = share * padded

    def body(place_ref, count_ref, keep_ref, patch_ref, grad_ref, gain_ref, shift_ref, *outs):
        tokens_ref, first_ref, rows_ref, sum_ref = outs
        image = place_ref[0] + pl.program_id(0)
        picks = slots_matrix(keep_ref[pl.ds(image, 1), :], patch_count)
        tokens = dot(picks, patch_ref[0], TN)
        tokens_ref[...] = tokens.astype(BF16)
        normal, _ = standard(tokens)
        first_ref[...] = (normal * gain_ref[...] + shift_ref[...]).astype(BF16)
        seen = lax.broadcasted_iota(jnp.int32, (slots, 1), 0) < count_ref[image]
        grads = jnp.where(seen, grad_ref[0].astype(F32), 0.0)
        rows_ref[...] = jnp.zeros_like(rows_ref)
        rows_ref[0:slots, :] = grads.astype(BF16)
        add_row(sum_ref, grads)

    return call(
        body,
        (share,),
        (place, counts),
        (keep, patches, out_grad, gain, shift),
        [
            full(keep.shape),
            pl.BlockSpec((1, patch_count, width), lambda i, p, c: (p[0] + i, 0, 0)),
            pl.BlockSpec((1, slots, width), lambda i, *_: (i, 0, 0)),
            full(gain.shape),
            full(shift.shape),
        ],
        (shape_of((total, width), BF16),) * 3 + (shape_of((1, width), F32),),
        [rows(padded, width)] * 3 + [full((1, width))],
        flops=2 * total * patch_count * width,
    )


def heads_of(width):
    lanes = lax.broadcasted_iota(jnp.int32, (1, width), 1) // HD
    return [(lanes == h).astype(BF16) for h in range(width // HD)]


def stacked(values, masks):
    return jnp.concatenate([values * m for m in masks], axis=0)


def merged(values, masks, length):
    lanes = lax.broadcasted_iota(jnp.int32, (1, values.shape[1]), 1) // HD
    result = values[0:length]
    for h in range(1, len(masks)):
        result = jnp.where(lanes == h, values[h * length : (h + 1) * length], result)
    return result


def probabilities(queries, keys, count, masks):
    scores = dot(stacked(queries, masks), keys, NT) * HD**-0.5
    seen = lax.broadcasted_iota(jnp.int32, (1, keys.shape[0]), 1) < count
    scores = jnp.where(seen, scores, MASKED)
    powers = jnp.exp(scores - jnp.max(scores, axis=-1, keepdims=True))
    return powers / jnp.sum(powers, axis=-1, keepdims=True)


def attend(place, counts, first, weights, bias, padded):
    total, width = first.shape
    inner = bias.shape[1]
    part = inner // 3
    group = 2

    def body(place_ref, count_ref, first_ref, w_ref, bias_ref, qkv_ref, out_ref):
        masks = heads_of(part)
        qkv = dot(first_ref[...], w_ref[...], NT) + bias_ref[...]
        qkv = qkv.astype(BF16)
        qkv_ref[...] = qkv
        for g in range(group):
            image = place_ref[0] + pl.program_id(0) * group + g
            block = qkv[g * padded : (g + 1) * padded]
            q, k, v = (block[:, j * part : (j + 1) * part] for j in range(3))
            chances = probabilities(q, k, count_ref[image], masks).astype(BF16)
            mixed = dot(chances, v)
            out_ref[g * padded : (g + 1) * padded, :] = merged(mixed, masks, padded).astype(BF16)

    size = group * padded
    return call(
        body,
        (total // size,),
        (place, counts),
        (first, weights, bias),
        [rows(size, width), full((inner, width)), full(bias.shape)],
        (shape_of((total, inner), BF16), shape_of((total, part), BF16)),
        [rows(size, inner), rows(size, part)],
        flops=2 * total * inner * width,
    )


def join(tokens, attended, weights, b_out, gain, shift, size):
    total, width = tokens.shape
    part = attended[0].shape[1]
    n = len(attended)

    def body(*refs):
        tokens_ref, refs = refs[0], refs[1:]
        att_refs, w_refs = refs[:n], refs[n : 2 * n]
        bias_ref, gain_ref, shift_ref, middle_ref, second_ref = refs[2 * n :]
        middle = tokens_ref[...].astype(F32) + bias_ref[...]
        branch = dot(att_refs[0][...], w_refs[0][...])
        for a, w in zip(att_refs[1:], w_refs[1:]):
            branch += dot(a[...], w[...])
        middle += branch
        middle_ref[...] = middle
        normal, _ = standard(middle)
        second_ref[...] = (normal * gain_ref[...] + shift_ref[...]).astype(BF16)

    last = width // part - 1
    return call(
        body,
        (total // size,),
        (),
        (tokens, *attended, *weights, b_out, gain, shift),
        [rows(size, width)]
        + [rows(size, part)] * n
        + [pl.BlockSpec((part, width), lambda i: (last, 0))] * n
        + [full((1, width))] * 3,
        (shape_of((total, width), F32), shape_of((total, width), BF16)),
        [rows(size, width)] * 2,
        flops=2 * total * width * width,
    )


def feed(second, grads, up, down, bias, before, size):
    total, width = second.shape
    units = up.shape[1]
    steps = total // size
    root = 0.5**0.5
    density = (2.0 * jnp.pi) ** -0.5

    def body(*refs):
        second_ref, grads_ref, up_ref, down_ref, bias_ref = refs[:5]
        refs = refs[5:]
        if before:
            out_before, back_before = refs[:2]
            refs = refs[2:]
        out_ref, back_ref, d_up_ref, d_down_ref, d_bias_ref, hidden_ref, inner_ref = refs
        for s in range(steps):
            here = slice(s * size, (s + 1) * size)
            u = dot(second_ref[here, :], up_ref[...]) + bias_ref[...]
            gh = dot(grads_ref[here, :], down_ref[...], NT)
            below = 0.5 + 0.5 * lax.erf(u * root)
            hidden = (u * below).astype(BF16)
            slope = below + u * (jnp.exp(-0.5 * u * u) * density)
            gi = (gh * slope).astype(BF16)
            hidden_ref[here, :] = hidden
            inner_ref[here, :] = gi
            row = jnp.sum(gi.astype(F32), axis=0, keepdims=True)
            d_bias_ref[...] = row if s == 0 else d_bias_ref[...] + row
            out = dot(hidden, down_ref[...])
            back = dot(gi, up_ref[...], NT)
            if before:
                out += out_before[here, :]
                back += back_before[here, :]
            out_ref[here, :] = out
            back_ref[here, :] = back
        d_down_ref[...] = dot(hidden_ref[...], grads_ref[...], TN).astype(BF16)
        d_up_ref[...] = dot(second_ref[...], inner_ref[...], TN).astype(BF16)

    ins = (second, grads, up, down, bias, *before)
    outs = (
        shape_of((total, width), F32),
        shape_of((total, width), F32),
        shape_of((width, units), BF16),
        shape_of((units, width), BF16),
        shape_of((1, units), F32),
    )
    return call(
        body,
        (1,),
        (),
        ins,
        [full(a.shape) for a in ins],
        outs,
        [full(o.shape) for o in outs],
        scratch=[VMEM((total, units), BF16), VMEM((total, units), BF16)],
        flops=12 * total * width * units,
        alias={5: 0, 6: 1} if before else None,
    )


def middle_back(place, counts, middle, back, grads, out, gain, b_fc2, padded, slots):
    total, width = middle.shape
    share = total // padded

    def body(place_ref, count_ref, middle_ref, back_ref, grads_ref, out_ref, gain_ref, bias_ref, *outs):
        grad_ref, round_ref, layer_ref, d_gain_ref, d_shift_ref, d_bias_ref = outs
        middle = middle_ref[...]
        back = back_ref[...]
        normal, inverse = standard(middle)
        grad = grads_ref[...].astype(F32) + norm_back(normal, inverse, gain_ref[...], back)
        grad_ref[...] = grad
        round_ref[...] = grad.astype(BF16)
        add_row(d_gain_ref, back * normal)
        add_row(d_shift_ref, back)
        add_row(d_bias_ref, grad)
        image = place_ref[0] + pl.program_id(0)
        layer = middle + out_ref[...] + bias_ref[...]
        seen = lax.broadcasted_iota(jnp.int32, (padded, 1), 0) < count_ref[image]
        layer_ref[0] = jnp.where(seen, layer, 0.0).astype(BF16)[0:slots]

    one = shape_of((1, width), F32)
    return call(
        body,
        (share,),
        (place, counts),
        (middle, back, grads, out, gain, b_fc2),
        [rows(padded, width)] * 4 + [full((1, width))] * 2,
        (
            shape_of((total, width), F32),
            shape_of((total, width), BF16),
            shape_of((share, slots, width), BF16),
            one,
            one,
            one,
        ),
        [rows(padded, width)] * 2
        + [pl.BlockSpec((1, slots, width), lambda i, *_: (i, 0, 0))]
        + [full((1, width))] * 3,
        flops=20 * total * width,
    )


def attend_back(place, counts, grad, weights, qkv, attended, first, before, padded):
    total, width = grad.shape
    inner, part = qkv.shape[1], attended.shape[1]
    share = total // padded

    def body(place_ref, count_ref, grad_ref, w_ref, qkv_ref, att_ref, first_ref, *refs):
        if before:
            before_ref, refs = refs[0], refs[1:]
        back_ref, d_w_ref, d_bias_ref, three_ref = refs
        masks = heads_of(part)
        for i in range(share):
            here = slice(i * padded, (i + 1) * padded)
            ga = dot(grad_ref[here, :], w_ref[inner:, :], NT).astype(BF16)
            q, k, v = (qkv_ref[here, j * part : (j + 1) * part] for j in range(3))
            exact = probabilities(q, k, count_ref[place_ref[0] + i], masks)
            ga_all = stacked(ga, masks)
            gp = dot(ga_all, v, NT)
            gs = exact * (gp - jnp.sum(exact * gp, axis=-1, keepdims=True))
            gs = gs.astype(BF16)
            gq = merged(dot(gs, k), masks, padded) * HD**-0.5
            gk = dot(gs, stacked(q, masks), TN) * HD**-0.5
            gv = dot(exact.astype(BF16), ga_all, TN)
            for j, value in enumerate((gq, gk, gv)):
                three_ref[here, j * part : (j + 1) * part] = value.astype(BF16)
            back = dot(three_ref[here, :], w_ref[:inner, :])
            if before:
                back += before_ref[here, :]
            back_ref[here, :] = back
        d_w_ref[:inner, :] = dot(three_ref[...], first_ref[...], TN).astype(BF16)
        d_w_ref[inner:, :] = dot(att_ref[...], grad_ref[...], TN).astype(BF16)
        d_bias_ref[...] = jnp.sum(three_ref[...].astype(F32), axis=0, keepdims=True)

    ins = (grad, weights, qkv, attended, first, *before)
    outs = (
        shape_of((total, width), F32),
        shape_of(weights.shape, BF16),
        shape_of((1, inner), F32),
    )
    return call(
        body,
        (1,),
        (place, counts),
        ins,
        [full(a.shape) for a in ins],
        outs,
        [full(o.shape) for o in outs],
        scratch=[VMEM((total, inner), BF16)],
        flops=6 * total * width * width,
        alias={7: 0} if before else None,
    )


def finish(place, keep, tokens, back, grad, gain, patch_count, padded):
    total, width = tokens.shape
    share = total // padded

    def body(place_ref, keep_ref, tokens_ref, back_ref, grad_ref, gain_ref, out_ref, d_gain_ref, d_shift_ref):
        back = back_ref[...]
        normal, inverse = standard(tokens_ref[...].astype(F32))
        grad = grad_ref[...] + norm_back(normal, inverse, gain_ref[...], back)
        add_row(d_gain_ref, back * normal)
        add_row(d_shift_ref, back)
        image = place_ref[0] + pl.program_id(0)
        picks = slots_matrix(keep_ref[pl.ds(image, 1), :], patch_count)
        high = grad.astype(BF16)
        low = (grad - high.astype(F32)).astype(BF16)
        out_ref[0] = dot(picks, high) + dot(picks, low)

    one = shape_of((1, width), F32)
    return call(
        body,
        (share,),
        (place,),
        (keep, tokens, back, grad, gain),
        [full(keep.shape)] + [rows(padded, width)] * 3 + [full((1, width))],
        (shape_of((share, patch_count, width), F32), one, one),
        [pl.BlockSpec((1, patch_count, width), lambda i, *_: (i, 0, 0))] + [full((1, width))] * 2,
        flops=4 * total * patch_count * width,
    )


def swap(value, axis, bit):
    size = lax.axis_size(axis)
    return lax.ppermute(value, axis, [(i, i ^ bit) for i in range(size)])


def after(value, *others):
    return lax.optimization_barrier((value, *others))[0]


def half(value, bit):
    size = value.shape[0] // 2
    return lax.dynamic_slice_in_dim(value, bit * size, size, 0)


def whole(mine, other, bit):
    return jnp.where(
        bit == 0, jnp.concatenate([mine, other], axis=0), jnp.concatenate([other, mine], axis=0)
    )


def place_bit(bit):
    return (lax.axis_index("dp") // bit) % 2


class Images:
    def __init__(self, value):
        self.value = value
        size = lax.axis_size("dp")
        bits = []
        while 2 ** len(bits) < size:
            bits.append(2 ** len(bits))
        self.steps = [("sum", bit) for bit in bits] + [("join", bit) for bit in reversed(bits)]
        self.sent = None
        self.start()

    def start(self):
        if not self.steps:
            return
        kind, bit = self.steps[0]
        if kind == "sum":
            outgoing = half(self.value, 1 - place_bit(bit)).astype(BF16)
            self.value = half(self.value, place_bit(bit))
        else:
            outgoing = self.value = self.value.astype(BF16)
        self.sent = swap(outgoing, "dp", bit)
        self.ready = outgoing

    def step(self, *others):
        if not self.steps:
            return self.value
        kind, bit = self.steps.pop(0)
        arrived = after(self.sent, *others) if others else self.sent
        if kind == "sum":
            self.value = self.value.astype(F32) + arrived.astype(F32)
        else:
            self.value = whole(self.value, arrived, place_bit(bit))
        self.start()
        return self.ready if self.steps else self.value

    def finish(self):
        while self.steps:
            self.step()
        return self.value.astype(F32)


def reduce_all(value):
    for axis in ("tensor", "dp"):
        bit = 1
        while bit < lax.axis_size(axis):
            value = value + swap(value, axis, bit)
            bit *= 2
    return value


def shards(
    patches,
    keep_slots,
    visible_count,
    gain_one,
    shift_one,
    w_qkv,
    b_qv,
    w_out,
    b_out,
    gain_two,
    shift_two,
    w_fc1,
    b_fc1,
    w_fc2,
    b_fc2,
    out_grad,
):
    images, slots = keep_slots.shape
    patch_count, width = patches.shape[1:]
    tensor = lax.axis_size("tensor")
    spot = lax.axis_index("tensor")
    share = images // tensor
    padded = -(-slots // 8) * 8
    part, units = w_qkv.shape[2], w_fc1.shape[1]
    inner = 3 * part
    begin = spot * share
    place = jnp.zeros((1,), jnp.int32)
    counts = lax.dynamic_slice_in_dim(visible_count, begin, share, 0)
    keep = lax.dynamic_slice_in_dim(keep_slots, begin, share, 0)
    keep = jnp.pad(keep, ((0, 0), (0, padded - slots)), constant_values=-1)
    patches = lax.dynamic_slice_in_dim(patches, begin, share, 0)
    line = lambda vector: vector.reshape(1, -1)
    side = place_bit(1)

    own = jnp.concatenate([w_qkv.transpose(0, 2, 1).reshape(inner, width), w_out], axis=0)
    far_mix = swap(half(own, side), "tensor", 2)
    near_mix = swap(own, "tensor", 1)
    biases = line(jnp.concatenate([b_qv[0], jnp.zeros_like(b_qv[0]), b_qv[1], b_fc1]))
    biases = jnp.concatenate([biases, swap(biases, "tensor", 1)], axis=0)
    biases = jnp.concatenate([biases, swap(biases, "tensor", 2)], axis=0)
    biases = [biases[r : r + 1] for r in range(tensor)]

    tokens, first, grad_rows, g_b_fc2 = prepare(
        place, counts, keep, patches, out_grad, line(gain_one), line(shift_one), slots
    )
    three, attended = [None] * 4, [None] * 4

    def attending(r, weights, *others):
        three[r], attended[r] = attend(
            place, counts, after(first, *others), weights, biases[r][:, :inner], padded
        )
        return attended[r]

    far_down = swap(half(after(w_fc2, first), side), "tensor", 2)
    done = attending(0, own)
    far_up = swap(after(w_fc1, done), "tensor", 2)
    done = attending(1, near_mix, done)
    far_mix = after(far_mix, done)
    far_mix = whole(far_mix, swap(far_mix, "dp", 1), side)
    cross_mix = swap(far_mix, "tensor", 1)
    done = attending(2, far_mix, done)
    done = attending(3, cross_mix, done)
    mixes = [own, near_mix, far_mix, cross_mix]
    far_down = after(far_down, done)
    far_down_other = swap(far_down, "dp", 1)
    near_up, near_down = (swap(after(w, done), "tensor", 1) for w in (w_fc1, w_fc2))
    middle, second = join(
        tokens, attended, mixes, line(b_out), line(gain_two), line(shift_two), 2 * padded
    )
    g_up, g_down, g_b_fc1 = [None] * 4, [None] * 4, [None] * 4
    before = ()

    def feeding(r, up, down, before, *others):
        out, back, g_up[r], g_down[r], g_b_fc1[r] = feed(
            after(second, *others), grad_rows, up, down, biases[r][:, inner:], before, 2 * padded
        )
        return out, back

    before = feeding(0, w_fc1, w_fc2, before)
    far_up = after(far_up, before[0])
    far_down = whole(far_down, after(far_down_other, before[0]), side)
    cross_up, cross_down = swap(far_up, "tensor", 1), swap(far_down, "tensor", 1)
    before = feeding(2, far_up, far_down, before)
    before = feeding(3, cross_up, cross_down, before)
    ends = [swap(g[3], "tensor", 1) for g in (g_up, g_down)]
    before = feeding(1, near_up, near_down, before)
    fars = [(g[2].astype(F32) + after(e, before[0]).astype(F32)).astype(BF16) for g, e in zip((g_up, g_down), ends)]
    fars = [swap(f, "tensor", 2) for f in fars]
    nears = [swap(g[1], "tensor", 1) for g in (g_up, g_down)]
    out, back = before
    grad_middle, grad_round, layer_out, g_gain_two, g_shift_two, g_b_out = middle_back(
        place, counts, middle, back, grad_rows, out, line(gain_two), line(b_fc2), padded, slots
    )
    g_mix, g_b_qkv = [None] * 4, [None] * 4

    def attending_back(r, before, *others):
        back, g_mix[r], g_b_qkv[r] = attend_back(
            place, counts, after(grad_round, *others), mixes[r], three[r], attended[r], first, before, padded
        )
        return (back,)

    before = attending_back(3, ())
    end = swap(g_mix[3], "tensor", 1)
    mine = [g[0].astype(F32) + n.astype(F32) for g, n in zip((g_up, g_down), nears)]
    one = Images(mine[0] + after(fars[0], before[0]).astype(F32))
    before = attending_back(2, before, one.ready)
    far = swap((g_mix[2].astype(F32) + after(end, before[0]).astype(F32)).astype(BF16), "tensor", 2)
    before = attending_back(1, before, one.step(before[0]))
    near = swap(g_mix[1], "tensor", 1)
    two = Images(mine[1] + after(fars[1], before[0]).astype(F32))
    before = attending_back(0, before, one.step(before[0]), two.ready)
    (back,) = before
    grad_patches, g_gain_one, g_shift_one = finish(
        place, keep, tokens, after(back, one.step(back), two.step(back)), grad_middle, line(gain_one), patch_count, padded
    )
    three = Images(g_mix[0].astype(F32) + near.astype(F32) + far.astype(F32))
    grad_w_fc1, grad_w_fc2, grad_mix = one.finish(), two.finish(), three.finish()
    shared = jnp.concatenate([g_gain_one, g_shift_one, g_b_out, g_gain_two, g_shift_two, g_b_fc2])
    local = jnp.concatenate([jnp.concatenate(g_b_qkv), jnp.concatenate(g_b_fc1)], axis=1)
    order = [lax.dynamic_slice_in_dim(local, spot ^ r, 1, 0) for r in range(tensor)]
    small = jnp.concatenate([shared.reshape(1, -1), jnp.concatenate(order, axis=0).reshape(1, -1)], axis=1)
    small = reduce_all(small)
    shared = small[0, : 6 * width].reshape(6, width)
    local = small[:, 6 * width :].reshape(tensor, inner + units)
    local = lax.dynamic_slice_in_dim(local, spot, 1, 0)[0]
    grad_b_qv = jnp.stack([local[:part], local[2 * part : inner]])
    grad_w_qkv = grad_mix[:inner].reshape(3, part, width).transpose(0, 2, 1)
    return (
        layer_out,
        grad_patches,
        shared[0],
        shared[1],
        grad_w_qkv,
        grad_b_qv,
        grad_mix[inner:],
        shared[2],
        shared[3],
        shared[4],
        grad_w_fc1,
        local[inner:],
        grad_w_fc2,
        shared[5],
    )


def solution(mesh):
    return jax.shard_map(
        shards,
        mesh=mesh,
        in_specs=(
            P("dp", None, None),
            P("dp", None),
            P("dp"),
            P(),
            P(),
            P(None, None, "tensor"),
            P(None, "tensor"),
            P("tensor", None),
            P(),
            P(),
            P(),
            P(None, "tensor"),
            P("tensor"),
            P("tensor", None),
            P(),
            P(("dp", "tensor"), None, None),
        ),
        out_specs=(
            P(("dp", "tensor"), None, None),
            P(("dp", "tensor"), None, None),
            P(),
            P(),
            P(None, None, "tensor"),
            P(None, "tensor"),
            P("tensor", None),
            P(),
            P(),
            P(),
            P(None, "tensor"),
            P("tensor"),
            P("tensor", None),
            P(),
        ),
        check_vma=False,
    )
```

time: 820 us -> 337 us (0.41)
  waiting for transfers between devices: 396 us -> 107 us
  other arithmetic: 156 us -> 35.8 us
  Pallas kernels: 0 us -> 120 us
  matrix products: 91 us -> 0 us
  local copies, waits for them, and re-layouts: 85.9 us -> 20.1 us
  blocking collectives: 63 us -> 0 us
  starting transfers between devices: 0.72 us -> 45 us
  between operations: 15.4 us -> 2.11 us
    psum x3 -> x0, waiting for transfers between devices: 383 us -> none  [the longest x1 141 us: shards(): middle = tokens + lax.psum(branch_part, 'tensor') + b_out]
    pallas_call x0 -> x16, Pallas kernels: none -> 120 us  [call(): pl.pallas_call(body, out_shape=outs, grid_spec=pltpu.PrefetchScalarGridSp...]
    ppermute x0 -> x45, waiting for transfers between devices: none -> 107 us  [swap(): return lax.ppermute(value, axis, [(i, i ^ bit) for i in range(size)])]
    dot_general x18 -> x0, matrix products: 91 us -> none  [the longest x1 15.7 us: shards(): jnp.einsum('ivf,df->ivd', grad_inner, w_fc1, preferred_element_type=jnp.f...]
    scatter-add x1 -> x0, other arithmetic: 81.4 us -> none  [shards(): grad_patches = jnp.zeros((share, patches.shape[1], patches.shape[2]), jnp...]
    psum x2 -> x0, blocking collectives: 63 us -> none  [the longest x1 41 us: shards(): lax.psum((grad_gain_one, grad_shift_one, grad_b_out, grad_gain_two, grad_...]
    gather x3 -> x0, local copies, waits for them, and re-layouts: 47.4 us -> none  [shards(): jnp.take_along_axis(patches, keep_slots[:, :, None], axis=1)]
    reduce_sum x15 -> x0, other arithmetic: 46 us -> none  [the longest x4 10.2 us: standard(): average = jnp.mean(inputs, axis=-1, keepdims=True)]
  transfers between devices with their start and end apart: 6 -> 45, of which waited for: 4 -> 18; matrix products, arithmetic and copies ran while one was open for 25% -> 14% of each run, Pallas kernels for 0% -> 36%
where the time goes in v1:
time: 337 us; the launch traced here: 330 us
  Pallas kernels  120 us (36%)
  waiting for transfers between devices  107 us (32%)
  starting transfers between devices  45 us (13%)
  other arithmetic  35.8 us (11%)
  local copies, waits for them, and re-layouts  20.1 us (6%)
    pallas_call x16, Pallas kernels, call(): pl.pallas_call(body, out_shape=outs, grid_spec=pltpu.PrefetchScalarGridSp...  120 us
    ppermute x45, waiting for transfers between devices, swap(): return lax.ppermute(value, axis, [(i, i ^ bit) for i in range(size)])  107 us
    ppermute x45, starting transfers between devices, swap(): return lax.ppermute(value, axis, [(i, i ^ bit) for i in range(size)])  45 us
  transfers between devices with their start and end apart: 45, of which 18 were waited for; matrix products, arithmetic and copies ran while one was open for 14% of the time, Pallas kernels for 36%

profile of v1, /device:TPU:0, one launch (start us, length us, event | category | flops | bytes accessed | tf_op | source)
XLA Modules:
  0.0 330.0 jit_solution(8458897776976396056)
XLA Ops:
  11.9 5.5 %shard_map.263 = (bf16[624,768]{1,0:T(8,128)(2,1)S(1)}, bf16[624,768]{1,0:T(8,128)(2,1)S(1)}, bf16[624,768]{1,0:T(8,128)(2,1)S(1)}, f32[1,768]{1,0:T(1,128)S(1)}) custom-call(s32[1]{0:T(128)} %constant.163.clone.1.place_ref, s32[6]{0:T(128)S(1)} %dynamic_slice.84.count_ref, s32[6,104]{1,0:T(8,128)S(1)} %pad.4.keep_ref, bf16[6,196,768]{2,1,0:T(8,128)(2,1)} %copy.40.patch_ref, ...), custom_call_target="tpu_custom_call" | custom-call | flops 18785894400 | bytes 559660800 | tf_op jit(solution)/shard_map/pallas_call | solution.py:66
  17.4 4.0 %shard_map.264 = (bf16[624,576]{1,0:T(8,128)(2,1)S(1)}, bf16[624,192]{1,0:T(8,128)(2,1)S(1)}) custom-call(s32[1]{0:T(128)} %constant.163.clone.1.place_ref, s32[6]{0:T(128)S(1)} %dynamic_slice.84.count_ref, bf16[624,768]{1,0:T(8,128)(2,1)S(1)} %get-tuple-element.101.first_ref, bf16[768,768]{1,0:T(8,128)(2,1)S(1)} %pad_maximum_fusion.w_ref.refs_5_, ...), custom_call_target="tpu_custom_call" | custom-call | flops 55207526400 | bytes 309888000 | tf_op jit(solution)/shard_map/pallas_call | solution.py:66
  35.1 16.3 %collective-permute-done.4 = f32[2,1344]{1,0:T(2,128)S(1)} collective-permute-done((f32[2,1344]{1,0:T(2,128)S(1)}, f32[2,1344]{1,0:T(2,128)S(1)}, u32[]{:S(2)}, u32[]{:S(2)}) %collective-permute-start.4) | collective-permute-done | bytes 10784 | tf_op jit(solution)/shard_map/ppermute | solution.py:397
  61.4 4.3 %shard_map.268 = (f32[624,768]{1,0:T(8,128)}, bf16[624,768]{1,0:T(8,128)(2,1)S(1)}) custom-call(bf16[624,768]{1,0:T(8,128)(2,1)S(1)} %copy-done.13, bf16[624,192]{1,0:T(8,128)(2,1)S(1)} %copy-done.24, bf16[624,192]{1,0:T(8,128)(2,1)S(1)} %copy-done.27, bf16[624,192]{1,0:T(8,128)(2,1)S(1)} %get-tuple-element.100.refs_3_.att_ref, ...), custom_call_target="tpu_custom_call" | custom-call | flops 73610035200 | bytes 952012800 | tf_op jit(solution)/shard_map/pallas_call | solution.py:66
  68.8 8.3 %shard_map.269 = (f32[624,768]{1,0:T(8,128)}, f32[624,768]{1,0:T(8,128)}, bf16[768,768]{1,0:T(8,128)(2,1)S(1)}, bf16[768,768]{1,0:T(8,128)(2,1)}, f32[1,768]{1,0:T(1,128)S(1)}) custom-call(bf16[624,768]{1,0:T(8,128)(2,1)S(1)} %get-tuple-element.104.refs_0_, bf16[624,768]{1,0:T(8,128)(2,1)S(1)} %get-tuple-element.105.refs_1_.grads_ref, ...), custom_call_target="tpu_custom_call" | custom-call | flops 441660211200 | bytes 1047552000 | tf_op jit(solution)/shard_map/pallas_call | solution.py:66
  77.3 5.7 %collective-permute-done.11 = bf16[384,768]{1,0:T(8,128)(2,1)} collective-permute-done((bf16[384,768]{1,0:T(8,128)(2,1)}, bf16[384,768]{1,0:T(8,128)(2,1)}, u32[]{:S(2)}, u32[]{:S(2)}) %collective-permute-start.11) | collective-permute-done | bytes 589856 | tf_op jit(solution)/shard_map/ppermute | solution.py:397
  85.9 8.9 %shard_map.270 = (f32[624,768]{1,0:T(8,128)}, f32[624,768]{1,0:T(8,128)}, bf16[768,768]{1,0:T(8,128)(2,1)S(1)}, bf16[768,768]{1,0:T(8,128)(2,1)}, f32[1,768]{1,0:T(1,128)S(1)}) custom-call(bf16[624,768]{1,0:T(8,128)(2,1)S(1)} %get-tuple-element.104.refs_0_, ...), custom_call_target="tpu_custom_call", output_to_operand_aliasing={{0}: (5, {}), {1}: (6, {})} | custom-call | flops 441660211200 | bytes 1430937600 | tf_op jit(solution)/shard_map/pallas_call | solution.py:66
  94.8 10.0 %shard_map.271 = (f32[624,768]{1,0:T(8,128)}, f32[624,768]{1,0:T(8,128)}, bf16[768,768]{1,0:T(8,128)(2,1)}, bf16[768,768]{1,0:T(8,128)(2,1)}, f32[1,768]{1,0:T(1,128)S(1)}) custom-call(bf16[624,768]{1,0:T(8,128)(2,1)S(1)} %get-tuple-element.104.refs_0_, ...), custom_call_target="tpu_custom_call", output_to_operand_aliasing={{0}: (5, {}), {1}: (6, {})} | custom-call | flops 441660211200 | bytes 1430937600 | tf_op jit(solution)/shard_map/pallas_call | solution.py:66
  105.3 9.6 %shard_map.272 = (f32[624,768]{1,0:T(8,128)}, f32[624,768]{1,0:T(8,128)}, bf16[768,768]{1,0:T(8,128)(2,1)}, bf16[768,768]{1,0:T(8,128)(2,1)}, f32[1,768]{1,0:T(1,128)S(1)}) custom-call(bf16[624,768]{1,0:T(8,128)(2,1)S(1)} %get-tuple-element.104.refs_0_, ...), custom_call_target="tpu_custom_call", output_to_operand_aliasing={{0}: (5, {}), {1}: (6, {})} | custom-call | flops 441660211200 | bytes 1430937600 | tf_op jit(solution)/shard_map/pallas_call | solution.py:66
  114.9 7.1 %shard_map.273 = (f32[624,768]{1,0:T(8,128)S(1)}, bf16[624,768]{1,0:T(8,128)(2,1)S(1)}, bf16[6,98,768]{2,1,0:T(8,128)(2,1)}, f32[1,768]{1,0:T(1,128)S(1)}, f32[1,768]{1,0:T(1,128)S(1)}, /*index=5*/f32[1,768]{1,0:T(1,128)S(1)}) custom-call(s32[1]{0:T(128)} %constant.163.clone.1.place_ref, s32[6]{0:T(128)S(1)} %dynamic_slice.84.count_ref, ...), custom_call_target="tpu_custom_call" | custom-call | flops 958464000 | bytes 1050316800 | tf_op jit(solution)/shard_map/pallas_call | solution.py:66
  125.8 10.2 %shard_map.274 = (f32[624,768]{1,0:T(8,128)}, bf16[768,768]{1,0:T(8,128)(2,1)}, f32[1,576]{1,0:T(1,128)S(1)}) custom-call(s32[1]{0:T(128)} %constant.163.clone.1.place_ref, s32[6]{0:T(128)S(1)} %dynamic_slice.84.count_ref, bf16[624,768]{1,0:T(8,128)(2,1)S(1)} %get-tuple-element.145.grad_ref, bf16[768,768]{1,0:T(8,128)(2,1)} %copy-done.10, ...), custom_call_target="tpu_custom_call" | custom-call | flops 220830105600 | bytes 715392000 | tf_op jit(solution)/shard_map/pallas_call | solution.py:66
  140.6 13.8 %collective-permute-done.15 = bf16[768,768]{1,0:T(8,128)(2,1)} collective-permute-done((bf16[768,768]{1,0:T(8,128)(2,1)}, bf16[768,768]{1,0:T(8,128)(2,1)}, u32[]{:S(2)}, u32[]{:S(2)}) %collective-permute-start.15) | collective-permute-done | bytes 1179680 | tf_op jit(solution)/shard_map/ppermute | solution.py:397
  159.2 11.0 %shard_map.275 = (f32[624,768]{1,0:T(8,128)}, bf16[768,768]{1,0:T(8,128)(2,1)}, f32[1,576]{1,0:T(1,128)S(1)}) custom-call(s32[1]{0:T(128)} %constant.163.clone.1.place_ref, s32[6]{0:T(128)S(1)} %dynamic_slice.84.count_ref, bf16[624,768]{1,0:T(8,128)(2,1)S(1)} %get-tuple-element.145.grad_ref, ...), custom_call_target="tpu_custom_call", output_to_operand_aliasing={{0}: (7, {})} | custom-call | flops 220830105600 | bytes 907084800 | tf_op jit(solution)/shard_map/pallas_call | solution.py:66
  177.5 10.8 %shard_map.276 = (f32[624,768]{1,0:T(8,128)}, bf16[768,768]{1,0:T(8,128)(2,1)}, f32[1,576]{1,0:T(1,128)S(1)}) custom-call(s32[1]{0:T(128)} %constant.163.clone.1.place_ref, s32[6]{0:T(128)S(1)} %dynamic_slice.84.count_ref, bf16[624,768]{1,0:T(8,128)(2,1)S(1)} %get-tuple-element.145.grad_ref, ...), custom_call_target="tpu_custom_call", output_to_operand_aliasing={{0}: (7, {})} | custom-call | flops 220830105600 | bytes 907084800 | tf_op jit(solution)/shard_map/pallas_call | solution.py:66
  197.0 11.1 %shard_map.277 = (f32[624,768]{1,0:T(8,128)}, bf16[768,768]{1,0:T(8,128)(2,1)}, f32[1,576]{1,0:T(1,128)S(1)}) custom-call(s32[1]{0:T(128)} %constant.163.clone.1.place_ref, s32[6]{0:T(128)S(1)} %dynamic_slice.84.count_ref, bf16[624,768]{1,0:T(8,128)(2,1)S(1)} %get-tuple-element.145.grad_ref, ...), custom_call_target="tpu_custom_call", output_to_operand_aliasing={{0}: (7, {})} | custom-call | flops 220830105600 | bytes 907084800 | tf_op jit(solution)/shard_map/pallas_call | solution.py:66
  213.2 7.0 %shard_map.278 = (f32[6,196,768]{2,1,0:T(8,128)}, f32[1,768]{1,0:T(1,128)S(1)}, f32[1,768]{1,0:T(1,128)S(1)}) custom-call(s32[1]{0:T(128)} %constant.163.clone.1.place_ref, s32[6,104]{1,0:T(8,128)S(1)} %copy-done.5, bf16[624,768]{1,0:T(8,128)(2,1)S(1)} %copy-done.14, f32[624,768]{1,0:T(8,128)S(1)} %copy-done.18, f32[624,768]{1,0:T(8,128)} %copy-done.8, ...), custom_call_target="tpu_custom_call" | custom-call | flops 37571788800 | bytes 841670400 | tf_op jit(solution)/shard_map/pallas_call | solution.py:66
  231.1 8.1 %collective-permute-done.25 = f32[1,9984]{1,0:T(1,128)S(1)} collective-permute-done((f32[1,9984]{1,0:T(1,128)S(1)}, f32[1,9984]{1,0:T(1,128)S(1)}, u32[]{:S(2)}, u32[]{:S(2)}) %collective-permute-start.25) | collective-permute-done | bytes 39968 | tf_op jit(solution)/shard_map/ppermute | solution.py:397
  247.5 6.3 %collective-permute-done.40 = bf16[192,768]{1,0:T(8,128)(2,1)S(1)} collective-permute-done((bf16[192,768]{1,0:T(8,128)(2,1)}, bf16[192,768]{1,0:T(8,128)(2,1)S(1)}, u32[]{:S(2)}, u32[]{:S(2)}) %collective-permute-start.40) | collective-permute-done | bytes 294944 | tf_op jit(solution)/shard_map/ppermute | solution.py:397
  256.3 5.7 %collective-permute-done.32 = bf16[192,768]{1,0:T(8,128)(2,1)S(1)} collective-permute-done((bf16[192,768]{1,0:T(8,128)(2,1)S(1)}, bf16[192,768]{1,0:T(8,128)(2,1)S(1)}, u32[]{:S(2)}, u32[]{:S(2)}) %collective-permute-start.32) | collective-permute-done | bytes 294944 | tf_op jit(solution)/shard_map/ppermute | solution.py:397
  265.2 8.8 %collective-permute-done.33 = bf16[96,768]{1,0:T(8,128)(2,1)S(1)} collective-permute-done((bf16[96,768]{1,0:T(8,128)(2,1)S(1)}, bf16[96,768]{1,0:T(8,128)(2,1)S(1)}, u32[]{:S(2)}, u32[]{:S(2)}) %collective-permute-start.33) | collective-permute-done | bytes 147488 | tf_op jit(solution)/shard_map/ppermute | solution.py:397
  276.1 4.2 %collective-permute-done.42 = bf16[96,768]{1,0:T(8,128)(2,1)S(1)} collective-permute-done((bf16[96,768]{1,0:T(8,128)(2,1)S(1)}, bf16[96,768]{1,0:T(8,128)(2,1)S(1)}, u32[]{:S(2)}, u32[]{:S(2)}) %collective-permute-start.42) | collective-permute-done | bytes 147488 | tf_op jit(solution)/shard_map/ppermute | solution.py:397
  283.0 5.0 %collective-permute-done.38 = bf16[192,768]{1,0:T(8,128)(2,1)S(1)} collective-permute-done((bf16[192,768]{1,0:T(8,128)(2,1)S(1)}, bf16[192,768]{1,0:T(8,128)(2,1)S(1)}, u32[]{:S(2)}, u32[]{:S(2)}) %collective-permute-start.38) | collective-permute-done | bytes 294944 | tf_op jit(solution)/shard_map/ppermute | solution.py:397
  306.8 11.0 %collective-permute-done.44 = bf16[384,768]{1,0:T(8,128)(2,1)S(1)} collective-permute-done((bf16[384,768]{1,0:T(8,128)(2,1)S(1)}, bf16[384,768]{1,0:T(8,128)(2,1)S(1)}, u32[]{:S(2)}, u32[]{:S(2)}) %collective-permute-start.44) | collective-permute-done | bytes 589856 | tf_op jit(solution)/shard_map/ppermute | solution.py:397
  319.4 7.7 %collective-permute-done.36 = bf16[384,768]{1,0:T(8,128)(2,1)S(1)} collective-permute-done((bf16[384,768]{1,0:T(8,128)(2,1)S(1)}, bf16[384,768]{1,0:T(8,128)(2,1)S(1)}, u32[]{:S(2)}, u32[]{:S(2)}) %collective-permute-start.36) | collective-permute-done | bytes 589856 | tf_op jit(solution)/shard_map/ppermute | solution.py:397
  (269 shorter events, 127.5 us)
Async XLA Ops:
  2.1 20.0 %collective-permute-start = (bf16[768,768]{1,0:T(8,128)(2,1)S(1)}, bf16[768,768]{1,0:T(8,128)(2,1)S(1)}, u32[]{:S(2)}, u32[]{:S(2)}) collective-permute-start(bf16[768,768]{1,0:T(8,128)(2,1)S(1)} %pad_maximum_fusion.w_ref.refs_5_), channel_id=1, source_target_pairs={{0,1},{1,0},{2,3},{3,2},{4,5},{5,4},{6,7},{7,6},{8,9},{9,8},{10,11... | collective-permute-start | bytes 3538952 | tf_op jit(solution)/shard_map/ppermute | solution.py:397
  2.8 19.3 %collective-permute-start.1 = (f32[1,1344]{1,0:T(1,128)S(1)}, f32[1,1344]{1,0:T(1,128)S(1)}, u32[]{:S(2)}, u32[]{:S(2)}) collective-permute-start(f32[1,1344]{1,0:T(1,128)S(1)} %reshape.86), channel_id=1, source_target_pairs={{0,1},{1,0},{2,3},{3,2},{4,5},{5,4},{6,7},{7,6},{8,9},{9,8},{10,11... | collective-permute-start | bytes 16136 | tf_op jit(solution)/shard_map/ppermute | solution.py:397
  4.0 23.8 %collective-permute-start.2 = (bf16[384,768]{1,0:T(8,128)(2,1)}, bf16[384,768]{1,0:T(8,128)(2,1)}, u32[]{:S(2)}, u32[]{:S(2)}) collective-permute-start(bf16[384,768]{1,0:T(8,128)(2,1)} %fusion.3), channel_id=1, source_target_pairs={{0,2},{1,3},{2,0},{3,1},{4,6},{5,7},{6,4},{7,5},{8,10},{9,11},{10,... | collective-permute-start | bytes 1769480 | tf_op jit(solution)/shard_map/ppermute | solution.py:397
  22.1 55.1 %collective-permute-start.8 = (bf16[768,768]{1,0:T(8,128)(2,1)}, bf16[768,768]{1,0:T(8,128)(2,1)}, u32[]{:S(2)}, u32[]{:S(2)}) collective-permute-start(bf16[768,768]{1,0:T(8,128)(2,1)} %refs_2_.1), channel_id=1, source_target_pairs={{0,2},{1,3},{2,0},{3,1},{4,6},{5,7},{6,4},{7,5},{8,10},{9,11},{10,... | collective-permute-start | bytes 3538952 | tf_op jit(solution)/shard_map/ppermute | solution.py:397
  27.8 23.7 %collective-permute-start.3 = (bf16[384,768]{1,0:T(8,128)(2,1)}, bf16[384,768]{1,0:T(8,128)(2,1)S(1)}, u32[]{:S(2)}, u32[]{:S(2)}) collective-permute-start(bf16[384,768]{1,0:T(8,128)(2,1)} %collective-permute-done.2), channel_id=1, source_target_pairs={{0,4},{4,0},{8,12},{12,8},{16,20},{20,16},{24,28},{28,24},{1,5},{5... | collective-permute-start | bytes 1769480 | tf_op jit(solution)/shard_map/ppermute | solution.py:397
  30.8 20.6 %collective-permute-start.4 = (f32[2,1344]{1,0:T(2,128)S(1)}, f32[2,1344]{1,0:T(2,128)S(1)}, u32[]{:S(2)}, u32[]{:S(2)}) collective-permute-start(f32[2,1344]{1,0:T(2,128)S(1)} %pad_maximum_fusion.2), channel_id=1, source_target_pairs={{0,2},{1,3},{2,0},{3,1},{4,6},{5,7},{6,4},{7,5},{8,10},{9,11},{10,... | collective-permute-start | bytes 32264 | tf_op jit(solution)/shard_map/ppermute | solution.py:397
  34.3 32.1 %collective-permute-start.10 = (bf16[384,768]{1,0:T(8,128)(2,1)}, bf16[384,768]{1,0:T(8,128)(2,1)}, u32[]{:S(2)}, u32[]{:S(2)}) collective-permute-start(bf16[384,768]{1,0:T(8,128)(2,1)} %constant_dynamic-slice_fusion.5), channel_id=1, source_target_pairs={{0,2},{1,3},{2,0},{3,1},{4,6},{5,7},{6,4},{7,5},{8,10},{9,11},{10,... | collective-permute-start | bytes 1769480 | tf_op jit(solution)/shard_map/ppermute | solution.py:397
  65.7 39.6 %collective-permute-start.6 = (bf16[768,768]{1,0:T(8,128)(2,1)}, bf16[768,768]{1,0:T(8,128)(2,1)}, u32[]{:S(2)}, u32[]{:S(2)}) collective-permute-start(bf16[768,768]{1,0:T(8,128)(2,1)} %refs_2_.1), channel_id=1, source_target_pairs={{0,1},{1,0},{2,3},{3,2},{4,5},{5,4},{6,7},{7,6},{8,9},{9,8},{10,11... | collective-permute-start | bytes 3538952 | tf_op jit(solution)/shard_map/ppermute | solution.py:397
  66.3 39.0 %collective-permute-start.7 = (bf16[768,768]{1,0:T(8,128)(2,1)}, bf16[768,768]{1,0:T(8,128)(2,1)}, u32[]{:S(2)}, u32[]{:S(2)}) collective-permute-start(bf16[768,768]{1,0:T(8,128)(2,1)} %refs_3_.1), channel_id=1, source_target_pairs={{0,1},{1,0},{2,3},{3,2},{4,5},{5,4},{6,7},{7,6},{8,9},{9,8},{10,11... | collective-permute-start | bytes 3538952 | tf_op jit(solution)/shard_map/ppermute | solution.py:397
  77.1 17.7 %collective-permute-start.9 = (bf16[768,768]{1,0:T(8,128)(2,1)}, bf16[768,768]{1,0:T(8,128)(2,1)}, u32[]{:S(2)}, u32[]{:S(2)}) collective-permute-start(bf16[768,768]{1,0:T(8,128)(2,1)} %collective-permute-done.8.refs_2_), channel_id=1, source_target_pairs={{0,1},{1,0},{2,3},{3,2},{4,5},{5,4},{6,7},{7,6},{8,9},{9,8},{10,11... | collective-permute-start | bytes 3538952 | tf_op jit(solution)/shard_map/ppermute | solution.py:397
  104.8 17.7 %collective-permute-start.14 = (bf16[768,768]{1,0:T(8,128)(2,1)}, bf16[768,768]{1,0:T(8,128)(2,1)}, u32[]{:S(2)}, u32[]{:S(2)}) collective-permute-start(bf16[768,768]{1,0:T(8,128)(2,1)} %get-tuple-element.126), channel_id=1, source_target_pairs={{0,1},{1,0},{2,3},{3,2},{4,5},{5,4},{6,7},{7,6},{8,9},{9,8},{10,11... | collective-permute-start | bytes 3538952 | tf_op jit(solution)/shard_map/ppermute | solution.py:397
  122.0 32.4 %collective-permute-start.13 = (bf16[768,768]{1,0:T(8,128)(2,1)}, bf16[768,768]{1,0:T(8,128)(2,1)}, u32[]{:S(2)}, u32[]{:S(2)}) collective-permute-start(bf16[768,768]{1,0:T(8,128)(2,1)} %get-tuple-element.124), channel_id=1, source_target_pairs={{0,1},{1,0},{2,3},{3,2},{4,5},{5,4},{6,7},{7,6},{8,9},{9,8},{10,11... | collective-permute-start | bytes 3538952 | tf_op jit(solution)/shard_map/ppermute | solution.py:397
  125.3 29.1 %collective-permute-start.15 = (bf16[768,768]{1,0:T(8,128)(2,1)}, bf16[768,768]{1,0:T(8,128)(2,1)}, u32[]{:S(2)}, u32[]{:S(2)}) collective-permute-start(bf16[768,768]{1,0:T(8,128)(2,1)} %add_convert_fusion.2), channel_id=1, source_target_pairs={{0,2},{1,3},{2,0},{3,1},{4,6},{5,7},{6,4},{7,5},{8,10},{9,11},{10,... | collective-permute-start | bytes 3538952 | tf_op jit(solution)/shard_map/ppermute | solution.py:397
  136.0 34.3 %collective-permute-start.29 = (bf16[768,768]{1,0:T(8,128)(2,1)}, bf16[768,768]{1,0:T(8,128)(2,1)}, u32[]{:S(2)}, u32[]{:S(2)}) collective-permute-start(bf16[768,768]{1,0:T(8,128)(2,1)} %get-tuple-element.170), channel_id=1, source_target_pairs={{0,1},{1,0},{2,3},{3,2},{4,5},{5,4},{6,7},{7,6},{8,9},{9,8},{10,11... | collective-permute-start | bytes 3538952 | tf_op jit(solution)/shard_map/ppermute | solution.py:397
  136.0 52.3 %collective-permute-start.18 = (bf16[768,768]{1,0:T(8,128)(2,1)}, bf16[768,768]{1,0:T(8,128)(2,1)}, u32[]{:S(2)}, u32[]{:S(2)}) collective-permute-start(bf16[768,768]{1,0:T(8,128)(2,1)} %get-tuple-element.140), channel_id=1, source_target_pairs={{0,1},{1,0},{2,3},{3,2},{4,5},{5,4},{6,7},{7,6},{8,9},{9,8},{10,11... | collective-permute-start | bytes 3538952 | tf_op jit(solution)/shard_map/ppermute | solution.py:397
  139.1 49.2 %collective-permute-start.20 = (bf16[768,768]{1,0:T(8,128)(2,1)}, bf16[768,768]{1,0:T(8,128)(2,1)}, u32[]{:S(2)}, u32[]{:S(2)}) collective-permute-start(bf16[768,768]{1,0:T(8,128)(2,1)} %add_convert_fusion.1), channel_id=1, source_target_pairs={{0,2},{1,3},{2,0},{3,1},{4,6},{5,7},{6,4},{7,5},{8,10},{9,11},{10,... | collective-permute-start | bytes 3538952 | tf_op jit(solution)/shard_map/ppermute | solution.py:397
  173.3 47.0 %collective-permute-start.30 = (bf16[768,768]{1,0:T(8,128)(2,1)}, bf16[768,768]{1,0:T(8,128)(2,1)}, u32[]{:S(2)}, u32[]{:S(2)}) collective-permute-start(bf16[768,768]{1,0:T(8,128)(2,1)} %add_convert_fusion), channel_id=1, source_target_pairs={{0,2},{1,3},{2,0},{3,1},{4,6},{5,7},{6,4},{7,5},{8,10},{9,11},{10,... | collective-permute-start | bytes 3538952 | tf_op jit(solution)/shard_map/ppermute | solution.py:397
  191.4 19.3 %collective-permute-start.22 = (bf16[384,768]{1,0:T(8,128)(2,1)}, bf16[384,768]{1,0:T(8,128)(2,1)}, u32[]{:S(2)}, u32[]{:S(2)}) collective-permute-start(bf16[384,768]{1,0:T(8,128)(2,1)} %dynamic-slice_convert_fusion.1), channel_id=1, source_target_pairs={{0,4},{4,0},{8,12},{12,8},{16,20},{20,16},{24,28},{28,24},{1,5},{5... | collective-permute-start | bytes 1769480 | tf_op jit(solution)/shard_map/ppermute | solution.py:397
  191.7 28.6 %collective-permute-start.28 = (bf16[768,768]{1,0:T(8,128)(2,1)}, bf16[768,768]{1,0:T(8,128)(2,1)}, u32[]{:S(2)}, u32[]{:S(2)}) collective-permute-start(bf16[768,768]{1,0:T(8,128)(2,1)} %get-tuple-element.168), channel_id=1, source_target_pairs={{0,1},{1,0},{2,3},{3,2},{4,5},{5,4},{6,7},{7,6},{8,9},{9,8},{10,11... | collective-permute-start | bytes 3538952 | tf_op jit(solution)/shard_map/ppermute | solution.py:397
  223.6 22.3 %collective-permute-start.31 = (bf16[384,768]{1,0:T(8,128)(2,1)}, bf16[384,768]{1,0:T(8,128)(2,1)}, u32[]{:S(2)}, u32[]{:S(2)}) collective-permute-start(bf16[384,768]{1,0:T(8,128)(2,1)} %dynamic-slice_convert_fusion), channel_id=1, source_target_pairs={{0,4},{4,0},{8,12},{12,8},{16,20},{20,16},{24,28},{28,24},{1,5},{5... | collective-permute-start | bytes 1769480 | tf_op jit(solution)/shard_map/ppermute | solution.py:397
  240.3 33.8 %collective-permute-start.37 = (bf16[96,768]{1,0:T(8,128)(2,1)}, bf16[96,768]{1,0:T(8,128)(2,1)S(1)}, u32[]{:S(2)}, u32[]{:S(2)}) collective-permute-start(bf16[96,768]{1,0:T(8,128)(2,1)} %add_convert_fusion.5), channel_id=1, source_target_pairs={{0,16},{4,20},{8,24},{12,28},{16,0},{20,4},{24,8},{28,12},{1,17},{... | collective-permute-start | bytes 442376 | tf_op jit(solution)/shard_map/ppermute | solution.py:397
  245.8 30.2 %collective-permute-start.27 = (f32[1,9984]{1,0:T(1,128)S(1)}, f32[1,9984]{1,0:T(1,128)S(1)}, u32[]{:S(2)}, u32[]{:S(2)}) collective-permute-start(f32[1,9984]{1,0:T(1,128)S(1)} %add.186), channel_id=1, source_target_pairs={{0,16},{4,20},{8,24},{12,28},{16,0},{20,4},{24,8},{28,12},{1,17},{... | collective-permute-start | bytes 119816 | tf_op jit(solution)/shard_map/ppermute | solution.py:397
  294.5 23.3 %collective-permute-start.44 = (bf16[384,768]{1,0:T(8,128)(2,1)S(1)}, bf16[384,768]{1,0:T(8,128)(2,1)S(1)}, u32[]{:S(2)}, u32[]{:S(2)}) collective-permute-start(bf16[384,768]{1,0:T(8,128)(2,1)S(1)} %maximum_select_fusion.7), channel_id=1, source_target_pairs={{0,4},{4,0},{8,12},{12,8},{16,20},{20,16},{24,28},{28,24},{1,5},{5... | collective-permute-start | bytes 1769480 | tf_op jit(solution)/shard_map/ppermute | solution.py:397
  298.9 28.2 %collective-permute-start.36 = (bf16[384,768]{1,0:T(8,128)(2,1)S(1)}, bf16[384,768]{1,0:T(8,128)(2,1)S(1)}, u32[]{:S(2)}, u32[]{:S(2)}) collective-permute-start(bf16[384,768]{1,0:T(8,128)(2,1)S(1)} %maximum_select_fusion.5), channel_id=1, source_target_pairs={{0,4},{4,0},{8,12},{12,8},{16,20},{20,16},{24,28},{28,24},{1,5},{5... | collective-permute-start | bytes 1769480 | tf_op jit(solution)/shard_map/ppermute | solution.py:397
  (74 other events, 511.1 us)
